TPU v7x, 32 devices: a whole 2x2x4 slice. The times are simulated.
32 devices in a mesh: groups: 2 (over y), span: 4 (over x, core), head: 4 (over z).
Axes of the slice: x: 2, y: 2, z: 4, core: 2. Of those that a mesh axis runs over, the one named last changes fastest.
Arguments:
- queries: bfloat16 [4096, 1024], P(('groups', 'span', 'head')), parts along dimension 0, may hold values from -8 to 8
- keys: bfloat16 [4096, 1024], P(('groups', 'span', 'head')), parts along dimension 0, may hold values from -8 to 8
- values: bfloat16 [4096, 1024], P(('groups', 'span', 'head')), parts along dimension 0, may hold values from -6 to 6
- tile_offsets: int32 [32, 7], P(('groups', 'span')), parts along dimension 0, may hold values from 0 to 6, as said below
- timesteps: int32 [8], P(('groups', 'span')), parts along dimension 0, may hold values from 0 to 999
- time_weight: bfloat16 [256, 1024], P(None, 'head'), may hold values from -0.375 to 0.375
Outputs:
- attended: bfloat16 [4096, 1024], P(('groups', 'span', 'head')), parts along dimension 0
There are 2 independent parts, one for each index of `groups`. A program takes and returns all parts, laid end to end along the dimension named above; an argument that names none is the same for every part. Nothing has to cross between parts.
Inputs may be any that keep to these rules, and one draw needn't show every extreme that they name: `tile_offsets`: the first entry of each row is 0 and the 7 entries of a row are distinct.
All inputs are finite; a program needn't handle non-finite values.
Results may differ from a plain program's by a relative error of at most 0.0035.
Values may be sent and summed in bfloat16 or wider, within the bound.
No kernel may reach another device: no remote copies, remote signals or barrier semaphores. Data moves between devices by JAX's collectives and lax.ppermute only.
A program may use at most 64 MiB of HBM per device.

v0:
```python
import math
import jax
import jax.numpy as jnp
from jax import lax
from jax.sharding import PartitionSpec as P

HEAD_SIZE = 128
TILE = 128
FREQ = 256


def shifted(value, axis, by):
    size = lax.axis_size(axis)
    pairs = [(i, i + by) for i in range(size) if 0 <= i + by < size]
    return lax.ppermute(value, axis, pairs)


def local(queries, keys, values, tile_offsets, timesteps, time_weight):
    query_heads, key_heads, value_heads = (
        lax.all_to_all(queries, "head", split_axis=1, concat_axis=0, tiled=True),
        lax.all_to_all(keys, "head", split_axis=1, concat_axis=0, tiled=True),
        lax.all_to_all(values, "head", split_axis=1, concat_axis=0, tiled=True),
    )
    span_rows = query_heads.shape[0]
    width = query_heads.shape[1]
    heads_here = width // HEAD_SIZE
    tiles_here = span_rows // TILE
    reach = 3 * tiles_here // 2
    listed = tile_offsets.shape[1]
    tail_rows = (reach - tiles_here) * TILE
    resident = jnp.concatenate([key_heads, value_heads], axis=1)
    nearer = shifted(resident, "span", 1)
    farther = shifted(resident[span_rows - tail_rows :], "span", 2)
    window = jnp.concatenate([farther, nearer, resident], axis=0)
    window = window.reshape(reach + tiles_here, TILE, 2 * width)
    half = FREQ // 2
    freqs = jnp.exp(-math.log(10000.0) * jnp.arange(half, dtype=jnp.float32) / half)
    angles = timesteps.astype(jnp.float32)[:, None] * freqs[None, :]
    embedded = jnp.concatenate([jnp.cos(angles), jnp.sin(angles)], axis=1)
    gate = jnp.dot(embedded, time_weight.astype(jnp.float32), precision=lax.Precision.HIGHEST)
    gate_rows = gate.reshape(1, 1, heads_here, HEAD_SIZE)
    position = lax.axis_index("span")
    scale = HEAD_SIZE ** (-0.5)
    query_blocks = query_heads.reshape(tiles_here // 4, 4, TILE, heads_here, HEAD_SIZE)
    offset_blocks = tile_offsets.reshape(tiles_here // 4, 4, listed)

    def one_block(inputs):
        block, query_part, offsets = inputs
        local_tiles = block * 4 + jnp.arange(4, dtype=jnp.int32)
        source = local_tiles[:, None] - offsets
        usable = position * tiles_here + source >= 0
        picked = window[source + reach].reshape(4, listed * TILE, 2 * width)
        key_part = picked[:, :, :width].reshape(4, listed * TILE, heads_here, HEAD_SIZE)
        value_part = picked[:, :, width:].reshape(4, listed * TILE, heads_here, HEAD_SIZE)
        scores = (
            jnp.einsum("qthd,qkhd->qhtk", query_part, key_part, preferred_element_type=jnp.float32)
            * scale
        )
        keep = jnp.repeat(usable, TILE, axis=1)
        scores = jnp.where(keep[:, None, None, :], scores, -1e30)
        top = jnp.max(scores, axis=-1, keepdims=True)
        weights = jnp.exp(scores - top)
        total = jnp.sum(weights, axis=-1, keepdims=True)
        rounded = weights.astype(jnp.bfloat16)
        mixed = jnp.einsum(
            "qhtk,qkhd->qthd", rounded, value_part, preferred_element_type=jnp.float32
        )
        mixed = mixed / jnp.transpose(total, (0, 2, 1, 3))
        return (mixed * (1.0 + gate_rows)).astype(jnp.bfloat16)

    blocks = jnp.arange(tiles_here // 4, dtype=jnp.int32)
    gated = lax.map(one_block, (blocks, query_blocks, offset_blocks)).reshape(span_rows, width)
    return lax.all_to_all(gated, "head", split_axis=0, concat_axis=1, tiled=True)


def solution(mesh):
    return jax.shard_map(
        local,
        mesh=mesh,
        in_specs=(
            P(("groups", "span", "head"), None),
            P(("groups", "span", "head"), None),
            P(("groups", "span", "head"), None),
            P(("groups", "span"), None),
            P(("groups", "span")),
            P(None, "head"),
        ),
        out_specs=P(("groups", "span", "head"), None),
        check_vma=False,
    )
```

profile of v0, /device:TPU:7, one launch (start us, length us, event | category | flops | bytes accessed | tf_op | source)
XLA Modules:
  0.0 76.2 jit_solution(9081810094877849396)
XLA Ops:
  0.0 0.0 copy-start
  0.0 0.0 copy-start.2
  0.0 1.8 %copy.18 = bf16[128,1024]{0,1:T(8,128)(2,1)} copy(bf16[128,1024]{1,0:T(8,128)(2,1)} %param.8) | data formatting | bytes 524288 | tf_op args[2]
  1.8 4.6 %all-to-all-start.1 = ((bf16[128,4,256]{0,2,1:T(8,128)(2,1)}), bf16[128,4,256]{0,2,1:T(8,128)(2,1)S(1)}, u32[]{:S(2)}, u32[]{:S(2)}) async-start(bf16[128,4,256]{0,2,1:T(8,128)(2,1)} %bitcast.3), calls=%async_computation.1 | async-start | bytes 524288 | tf_op jit(solution)/shard_map/all_to_all | solution.py:22
  6.4 1.8 %copy.16 = bf16[128,1024]{0,1:T(8,128)(2,1)} copy(bf16[128,1024]{1,0:T(8,128)(2,1)} %param.7) | data formatting | bytes 524288 | tf_op args[1]
  8.2 0.7 add_compare_fusion
  8.9 5.1 %all-to-all-done.1 = bf16[128,4,256]{0,2,1:T(8,128)(2,1)S(1)} async-done(((bf16[128,4,256]{0,2,1:T(8,128)(2,1)}), bf16[128,4,256]{0,2,1:T(8,128)(2,1)S(1)}, u32[]{:S(2)}, u32[]{:S(2)}) %all-to-all-start.1) | async-done | bytes 262176 | tf_op jit(solution)/shard_map/all_to_all | solution.py:22
  14.0 3.4 %all-to-all-start = ((bf16[128,4,256]{0,2,1:T(8,128)(2,1)}), bf16[128,4,256]{0,2,1:T(8,128)(2,1)S(1)}, u32[]{:S(2)}, u32[]{:S(2)}) async-start(bf16[128,4,256]{0,2,1:T(8,128)(2,1)} %bitcast), calls=%async_computation | async-start | bytes 524288 | tf_op jit(solution)/shard_map/all_to_all | solution.py:21
  17.4 0.1 broadcast_bitcast_fusion
  17.5 1.8 %copy.22 = bf16[128,1024]{0,1:T(8,128)(2,1)} copy(bf16[128,1024]{1,0:T(8,128)(2,1)} %param.6) | data formatting | bytes 524288 | tf_op args[0]
  19.9 0.1 fusion.27
  20.0 0.0 copy-done
  20.0 0.1 fusion.22
  20.1 0.2 copy.19
  20.3 2.7 %all-to-all-done = bf16[128,4,256]{0,2,1:T(8,128)(2,1)S(1)} async-done(((bf16[128,4,256]{0,2,1:T(8,128)(2,1)}), bf16[128,4,256]{0,2,1:T(8,128)(2,1)S(1)}, u32[]{:S(2)}, u32[]{:S(2)}) %all-to-all-start) | async-done | bytes 262176 | tf_op jit(solution)/shard_map/all_to_all | solution.py:21
  23.0 3.4 %all-to-all-start.2 = ((bf16[128,4,256]{0,2,1:T(8,128)(2,1)}), bf16[128,4,256]{0,2,1:T(8,128)(2,1)S(1)}, u32[]{:S(2)}, u32[]{:S(2)}) async-start(bf16[128,4,256]{0,2,1:T(8,128)(2,1)} %bitcast.10), calls=%async_computation.2 | async-start | bytes 524288 | tf_op jit(solution)/shard_map/all_to_all | solution.py:20
  26.4 0.1 copy.17
  26.6 1.3 %collective-permute-start.1 = (bf16[512,512]{1,0:T(8,128)(2,1)S(1)}, bf16[512,512]{1,0:T(8,128)(2,1)S(1)}, u32[]{:S(2)}, u32[]{:S(2)}) collective-permute-start(bf16[512,512]{1,0:T(8,128)(2,1)S(1)} %pad_maximum_fusion), channel_id=1, source_target_pairs={{0,4},{4,8},{8,12},{1,5},{5,9},{9,13},{2,6},{6,10},{10,14},{3,7},{... | collective-permute-start | bytes 1572872 | tf_op jit(solution)/shard_map/ppermute | solution.py:15
  27.9 0.0 copy-done.2
  27.9 0.1 reshape.97
  28.1 1.3 %collective-permute-start = (bf16[256,512]{1,0:T(8,128)(2,1)S(1)}, bf16[256,512]{1,0:T(8,128)(2,1)S(1)}, u32[]{:S(2)}, u32[]{:S(2)}) collective-permute-start(bf16[256,512]{1,0:T(8,128)(2,1)S(1)} %fusion.21), channel_id=1, source_target_pairs={{0,8},{4,12},{1,9},{5,13},{2,10},{6,14},{3,11},{7,15},{16,24},{20,... | collective-permute-start | bytes 786440 | tf_op jit(solution)/shard_map/ppermute | solution.py:15
  29.4 16.3 %collective-permute-done = bf16[256,512]{1,0:T(8,128)(2,1)S(1)} collective-permute-done((bf16[256,512]{1,0:T(8,128)(2,1)S(1)}, bf16[256,512]{1,0:T(8,128)(2,1)S(1)}, u32[]{:S(2)}, u32[]{:S(2)}) %collective-permute-start) | collective-permute-done | bytes 262176 | tf_op jit(solution)/shard_map/ppermute | solution.py:15
  45.7 0.0 collective-permute-done.1
  45.7 0.1 maximum_maximum_fusion
  45.8 2.6 %gather_fusion = bf16[28,128,512]{2,1,0:T(8,128)(2,1)} fusion(bf16[10,128,512]{2,1,0:T(8,128)(2,1)S(1)} %bitcast.73, s32[1024]{0:T(1024)S(1)} %pad_clamp_fusion), kind=kCustom, calls=%fused_computation | custom fusion | bytes 7340144 | tf_op jit(solution)/shard_map/while/body/eval_jaxpr/gather | solution.py:52
  48.5 3.6 %fusion.32 = (bf16[4,896,256]{2,1,0:T(8,128)(2,1)S(1)}, bf16[4,896,256]{2,1,0:T(8,128)(2,1)}) fusion(bf16[4,896,512]{2,1,0:T(8,128)(2,1)} %bitcast.74), kind=kLoop, calls=%fused_computation.40 | loop fusion | bytes 7340032 | tf_op jit(solution)/shard_map/while/body/eval_jaxpr/slice | solution.py:53
  52.0 3.6 %copy.20 = bf16[4,896,256]{1,2,0:T(8,128)(2,1)} copy(bf16[4,896,256]{2,1,0:T(8,128)(2,1)} %get-tuple-element.18) | data formatting | bytes 3670016 | tf_op jit(solution)/shard_map/while/body/eval_jaxpr/slice | solution.py:54
  55.6 2.4 %copy.21 = bf16[4,896,256]{1,2,0:T(8,128)(2,1)} copy(bf16[4,896,256]{2,1,0:T(8,128)(2,1)S(1)} %get-tuple-element.17) | data formatting | bytes 3670016 | tf_op jit(solution)/shard_map/while/body/eval_jaxpr/slice | solution.py:53
  58.0 0.0 all-to-all-done.2
  58.0 0.0 copy-start.1
  58.0 2.6 %bitcast_reduce_fusion = (f32[4,2,128]{2,1,0:T(2,128)S(1)}, f32[4,2,896,128]{3,2,1,0:T(8,128)S(1)}) fusion(pred[4,896]{1,0:T(4,128)(4,1)S(1)} %bitcast.88, bf16[4,896,2,128]{1,3,2,0:T(8,128)(2,1)} %bitcast.75, bf16[4,128,2,128]{1,3,2,0:T(8,128)(2,1)S(1)} %bitcast.86), kind=kOutput, calls=%fused_computation.2 | convolution fusion | flops 237632512 | bytes 5774848 | tf_op jit(solution)/shard_map/while/body/eval_jaxpr/qthd,qkhd->qhtk/dot_general | solution.py:56
  60.6 1.1 %fusion.1 = f32[4,2,128]{2,1,0:T(2,128)S(1)} fusion(f32[4,2,896,128]{3,2,1,0:T(8,128)S(1)} %get-tuple-element.20, f32[4,2,128]{2,1,0:T(2,128)S(1)} %get-tuple-element.19, pred[4,896]{1,0:T(4,128)(4,1)S(1)} %bitcast.89), kind=kLoop, calls=%fused_computation.5 | loop fusion | flops 3668992 | bytes 3681792 | tf_op jit(solution)/shard_map/while/body/eval_jaxpr/reduce_sum | solution.py:63
  61.7 0.0 copy-done.1
  61.7 1.3 %fusion.18 = bf16[4,128,2,128]{1,3,2,0:T(8,128)(2,1)S(1)} fusion(bf16[4,896,2,128]{1,3,2,0:T(8,128)(2,1)S(1)} %bitcast.82, f32[4,2,896,128]{3,2,1,0:T(8,128)S(1)} %get-tuple-element.20, f32[4,2,128]{2,1,0:T(2,128)S(1)} %get-tuple-element.19, pred[4,896]{1,0:T(4,128)(4,1)S(1)} %bitcast.90, f32[2,128]{1,0:T(2,128)S(1)} %broadcast_add_fusion, ...), kind=kOutput, calls=%fused_computation.16 | convolution fusion | flops 238944256 | bytes 5779968 | tf_op jit(solution)/shard_map/while/body/eval_jaxpr/qhtk,qkhd->qthd/dot_general | solution.py:65
  63.0 12.3 %all_to_all.73 = bf16[4,128,256]{1,2,0:T(8,128)(2,1)S(1)} all-to-all(bf16[4,128,256]{1,2,0:T(8,128)(2,1)S(1)} %bitcast.87), channel_id=1, replica_groups=mesh['groups'=2,'span'=4,'head'=4] {'head'}, dimensions={0} | all-to-all | bytes 524288 | tf_op jit(solution)/shard_map/all_to_all | solution.py:73
  75.4 0.8 %copy.32 = bf16[128,1024]{1,0:T(8,128)(2,1)} copy(bf16[128,1024]{0,1:T(8,128)(2,1)S(1)} %bitcast.85) | data formatting | bytes 524288 | tf_op jit(solution)/shard_map/all_to_all | solution.py:73
  (6 shorter events, 0.1 us)
Async XLA Ops:
  0.0 20.0 %copy-start = (bf16[256,256]{1,0:T(8,128)(2,1)S(1)}, bf16[256,256]{1,0:T(8,128)(2,1)}, u32[]{:S(2)}) copy-start(bf16[256,256]{1,0:T(8,128)(2,1)} %param.11) | copy-start | bytes 393220
  0.0 27.9 %copy-start.2 = (s32[4,7]{1,0:T(4,128)S(1)}, s32[4,7]{1,0:T(4,128)}, u32[]{:S(2)}) copy-start(s32[4,7]{1,0:T(4,128)} %param.9) | copy-start | bytes 340
  1.8 12.2 %all-to-all-start.1 = ((bf16[128,4,256]{0,2,1:T(8,128)(2,1)}), bf16[128,4,256]{0,2,1:T(8,128)(2,1)S(1)}, u32[]{:S(2)}, u32[]{:S(2)}) async-start(bf16[128,4,256]{0,2,1:T(8,128)(2,1)} %bitcast.3), calls=%async_computation.1 | async-start | bytes 524288 | tf_op jit(solution)/shard_map/all_to_all | solution.py:22
  14.0 9.0 %all-to-all-start = ((bf16[128,4,256]{0,2,1:T(8,128)(2,1)}), bf16[128,4,256]{0,2,1:T(8,128)(2,1)S(1)}, u32[]{:S(2)}, u32[]{:S(2)}) async-start(bf16[128,4,256]{0,2,1:T(8,128)(2,1)} %bitcast), calls=%async_computation | async-start | bytes 524288 | tf_op jit(solution)/shard_map/all_to_all | solution.py:21
  23.0 35.0 %all-to-all-start.2 = ((bf16[128,4,256]{0,2,1:T(8,128)(2,1)}), bf16[128,4,256]{0,2,1:T(8,128)(2,1)S(1)}, u32[]{:S(2)}, u32[]{:S(2)}) async-start(bf16[128,4,256]{0,2,1:T(8,128)(2,1)} %bitcast.10), calls=%async_computation.2 | async-start | bytes 524288 | tf_op jit(solution)/shard_map/all_to_all | solution.py:20
  26.6 19.1 %collective-permute-start.1 = (bf16[512,512]{1,0:T(8,128)(2,1)S(1)}, bf16[512,512]{1,0:T(8,128)(2,1)S(1)}, u32[]{:S(2)}, u32[]{:S(2)}) collective-permute-start(bf16[512,512]{1,0:T(8,128)(2,1)S(1)} %pad_maximum_fusion), channel_id=1, source_target_pairs={{0,4},{4,8},{8,12},{1,5},{5,9},{9,13},{2,6},{6,10},{10,14},{3,7},{... | collective-permute-start | bytes 1572872 | tf_op jit(solution)/shard_map/ppermute | solution.py:15
  28.1 17.7 %collective-permute-start = (bf16[256,512]{1,0:T(8,128)(2,1)S(1)}, bf16[256,512]{1,0:T(8,128)(2,1)S(1)}, u32[]{:S(2)}, u32[]{:S(2)}) collective-permute-start(bf16[256,512]{1,0:T(8,128)(2,1)S(1)} %fusion.21), channel_id=1, source_target_pairs={{0,8},{4,12},{1,9},{5,13},{2,10},{6,14},{3,11},{7,15},{16,24},{20,... | collective-permute-start | bytes 786440 | tf_op jit(solution)/shard_map/ppermute | solution.py:15
  58.0 3.8 %copy-start.1 = (bf16[4,896,256]{1,2,0:T(8,128)(2,1)S(1)}, bf16[4,896,256]{1,2,0:T(8,128)(2,1)}, u32[]{:S(2)}) copy-start(bf16[4,896,256]{1,2,0:T(8,128)(2,1)} %copy.20) | copy-start | bytes 5505028
where the time goes:
time: 76.8 us; the launch traced here: 76.2 us
  waiting for transfers between devices  24.1 us (31%)
  local copies, waits for them, and re-layouts  18.9 us (25%)
  starting transfers between devices  14 us (18%)
  blocking collectives  12.3 us (16%)
  matrix products  4.02 us (5%)
  other arithmetic  2.02 us (3%)
  between operations  0.81 us (1%)
    ppermute x2, waiting for transfers between devices, shifted(): return lax.ppermute(value, axis, pairs)  16.3 us
    all_to_all x1, blocking collectives, local(): lax.all_to_all(gated, 'head', split_axis=0, concat_axis=1, tiled=True)  12.3 us
    slice x2, local copies, waits for them, and re-layouts, one_block(): picked[:, :, :width].reshape(4, listed * TILE, heads_here, HEAD_SIZE)  5.92 us
    unnamed x11, local copies, waits for them, and re-layouts  5.49 us
    all_to_all x1, waiting for transfers between devices, local(): lax.all_to_all(values, 'head', split_axis=1, concat_axis=0, tiled=True)  5.09 us
    all_to_all x1, starting transfers between devices, local(): lax.all_to_all(values, 'head', split_axis=1, concat_axis=0, tiled=True)  4.59 us
    slice x1, local copies, waits for them, and re-layouts, one_block(): picked[:, :, width:].reshape(4, listed * TILE, heads_here, HEAD_SIZE)  3.6 us
    all_to_all x1, starting transfers between devices, local(): lax.all_to_all(queries, 'head', split_axis=1, concat_axis=0, tiled=True)  3.41 us
  transfers between devices with their start and end apart: 5, of which 3 were waited for; matrix products, arithmetic and copies ran while one was open for 23% of the time, Pallas kernels for 0%

commit v1 on v0

--- a/solution.py
+++ b/solution.py
@@ -9,6 +9,27 @@
 FREQ = 256
 
 
+def zones_take(net_axis, local_array):
+    response, w_next = (jax.lax.psum(1, net_axis), jax.lax.axis_index(net_axis))
+    block_next = local_array.shape[1] // response
+    current_arr = jnp.roll(local_array, -w_next * block_next, axis=1)
+    dev_j = 1
+    log = [lax.slice_in_dim(current_arr, 0, block_next, axis=1)]
+    while dev_j < response:
+        found_now = lax.slice_in_dim(
+            current_arr, dev_j * block_next, (dev_j + 1) * block_next, axis=1
+        )
+        log.append(
+            jax.lax.ppermute(
+                found_now, net_axis, [(no, (no + dev_j) % response) for no in range(response)]
+            )
+        )
+        dev_j += 1
+    current_block = jnp.concatenate(log[::-1], axis=0)
+    answer = jnp.roll(current_block, (w_next + 1) * log[0].shape[0], axis=0)
+    return answer
+
+
 def shifted(value, axis, by):
     size = lax.axis_size(axis)
     pairs = [(i, i + by) for i in range(size) if 0 <= i + by < size]
@@ -18,7 +39,7 @@
 def local(queries, keys, values, tile_offsets, timesteps, time_weight):
     query_heads, key_heads, value_heads = (
         lax.all_to_all(queries, "head", split_axis=1, concat_axis=0, tiled=True),
-        lax.all_to_all(keys, "head", split_axis=1, concat_axis=0, tiled=True),
+        zones_take("head", keys),
         lax.all_to_all(values, "head", split_axis=1, concat_axis=0, tiled=True),
     )
     span_rows = query_heads.shape[0]

time: 76.8 us -> 72.1 us (0.939)
  waiting for transfers between devices: 24.1 us -> 19.7 us
  local copies, waits for them, and re-layouts: 18.9 us -> 17.1 us
  other arithmetic: 2.02 us -> 3.08 us
    ppermute x0 -> x3, waiting for transfers between devices: none -> 5.34 us  [zones_take(): jax.lax.ppermute(found_now, net_axis, [(no, (no + dev_j) % response) for...]
    all_to_all x1, waiting for transfers between devices: 5.09 us -> 0.01 us  [local(): lax.all_to_all(values, 'head', split_axis=1, concat_axis=0, tiled=True)]
    ppermute x0 -> x3, starting transfers between devices: none -> 3.9 us  [zones_take(): jax.lax.ppermute(found_now, net_axis, [(no, (no + dev_j) % response) for...]
    all_to_all x1 -> x0, starting transfers between devices: 3.4 us -> none  [local(): lax.all_to_all(keys, 'head', split_axis=1, concat_axis=0, tiled=True)]
    all_to_all x1 -> x0, waiting for transfers between devices: 2.69 us -> none  [local(): lax.all_to_all(keys, 'head', split_axis=1, concat_axis=0, tiled=True)]
    unnamed x11 -> x17, local copies, waits for them, and re-layouts: 5.49 us -> 3.14 us
    ppermute x2, waiting for transfers between devices: 16.3 us -> 14.3 us  [shifted(): return lax.ppermute(value, axis, pairs)]
    concatenate x0 -> x1, other arithmetic: none -> 1.05 us  [zones_take(): current_arr = jnp.roll(local_array, -w_next * block_next, axis=1)]
  transfers between devices with their start and end apart: 5 -> 7, of which waited for: 3 -> 2; matrix products, arithmetic and copies ran while one was open for 23% -> 23% of each run, Pallas kernels for 0% -> 0%
where the time goes in v1:
time: 72.1 us; the launch traced here: 71.6 us
  waiting for transfers between devices  19.7 us (27%)
  local copies, waits for them, and re-layouts  17.1 us (24%)
  starting transfers between devices  14.5 us (20%)
  blocking collectives  12.3 us (17%)
  matrix products  4.02 us (6%)
  other arithmetic  3.08 us (4%)
  between operations  0.88 us (1%)
    ppermute x2, waiting for transfers between devices, shifted(): return lax.ppermute(value, axis, pairs)  14.3 us
    all_to_all x1, blocking collectives, local(): lax.all_to_all(gated, 'head', split_axis=0, concat_axis=1, tiled=True)  12.3 us
    slice x2, local copies, waits for them, and re-layouts, one_block(): picked[:, :, :width].reshape(4, listed * TILE, heads_here, HEAD_SIZE)  5.89 us
    ppermute x3, waiting for transfers between devices, zones_take(): jax.lax.ppermute(found_now, net_axis, [(no, (no + dev_j) % response) for...  5.34 us
    all_to_all x1, starting transfers between devices, local(): lax.all_to_all(values, 'head', split_axis=1, concat_axis=0, tiled=True)  4.59 us
    ppermute x3, starting transfers between devices, zones_take(): jax.lax.ppermute(found_now, net_axis, [(no, (no + dev_j) % response) for...  3.9 us
    slice x1, local copies, waits for them, and re-layouts, one_block(): picked[:, :, width:].reshape(4, listed * TILE, heads_here, HEAD_SIZE)  3.56 us
    all_to_all x1, starting transfers between devices, local(): lax.all_to_all(queries, 'head', split_axis=1, concat_axis=0, tiled=True)  3.42 us
  transfers between devices with their start and end apart: 7, of which 2 were waited for; matrix products, arithmetic and copies ran while one was open for 23% of the time, Pallas kernels for 0%

profile of v1, /device:TPU:7, one launch (start us, length us, event | category | flops | bytes accessed | tf_op | source)
XLA Modules:
  0.0 71.6 jit_solution(5152904601564752032)
XLA Ops:
  0.0 0.0 copy-start
  0.0 0.0 copy-start.2
  0.0 1.2 %copy.25 = bf16[128,1024]{0,1:T(8,128)(2,1)S(1)} copy(bf16[128,1024]{1,0:T(8,128)(2,1)} %param.8) | data formatting | bytes 524288 | tf_op args[2]
  1.2 0.9 %copy.26 = bf16[128,4,256]{2,0,1:T(8,128)(2,1)} copy(bf16[128,4,256]{0,2,1:T(8,128)(2,1)S(1)} %bitcast.79) | data formatting | bytes 524288 | tf_op jit(solution)/shard_map/all_to_all | solution.py:43
  2.0 4.6 %all-to-all-start = ((bf16[128,4,256]{2,0,1:T(8,128)(2,1)}), bf16[128,4,256]{2,0,1:T(8,128)(2,1)S(1)}, u32[]{:S(2)}, u32[]{:S(2)}) async-start(bf16[128,4,256]{2,0,1:T(8,128)(2,1)} %copy.26), calls=%async_computation | async-start | bytes 524288 | tf_op jit(solution)/shard_map/all_to_all | solution.py:43
  6.6 1.1 %fusion.21 = bf16[128,1024]{1,0:T(8,128)(2,1)S(1)} fusion(s32[]{:T(128)S(6)} %select_n.40, bf16[128,1024]{1,0:T(8,128)(2,1)} %param.7), kind=kLoop, calls=%fused_computation.22 | loop fusion | flops 524288 | bytes 524292 | tf_op jit(solution)/shard_map/jit(_roll_dynamic)/concatenate | solution.py:15
  7.7 3.3 %collective-permute-start = (bf16[128,256]{1,0:T(8,128)(2,1)S(1)}, bf16[128,256]{1,0:T(8,128)(2,1)S(1)}, u32[]{:S(2)}, u32[]{:S(2)}) collective-permute-start(bf16[128,256]{1,0:T(8,128)(2,1)S(1)} %get-tuple-element.28), channel_id=1, source_target_pairs={{0,3},{1,0},{2,1},{3,2},{4,7},{5,4},{6,5},{7,6},{8,11},{9,8},{10,9... | collective-permute-start | bytes 196616 | tf_op jit(solution)/shard_map/ppermute | solution.py:23
  11.0 0.0 collective-permute-start.1
  11.0 0.6 collective-permute-start.2
  12.2 0.1 fusion.28
  12.3 0.7 add_compare_fusion
  13.0 0.0 copy-done
  13.0 0.1 fusion.23
  13.1 0.1 broadcast_bitcast_fusion
  13.2 1.9 %copy.29 = bf16[128,1024]{0,1:T(8,128)(2,1)} copy(bf16[128,1024]{1,0:T(8,128)(2,1)} %param.6) | data formatting | bytes 524288 | tf_op args[0]
  15.1 0.0 collective-permute-done
  15.1 5.3 %collective-permute-done.1 = bf16[128,256]{1,0:T(8,128)(2,1)S(1)} collective-permute-done((bf16[128,256]{1,0:T(8,128)(2,1)S(1)}, bf16[128,256]{1,0:T(8,128)(2,1)S(1)}, u32[]{:S(2)}, u32[]{:S(2)}) %collective-permute-start.1) | collective-permute-done | bytes 65568 | tf_op jit(solution)/shard_map/ppermute | solution.py:23
  20.4 0.0 collective-permute-done.2
  20.6 0.0 all-to-all-done
  20.6 3.4 %all-to-all-start.1 = ((bf16[128,4,256]{0,2,1:T(8,128)(2,1)}), bf16[128,4,256]{0,2,1:T(8,128)(2,1)S(1)}, u32[]{:S(2)}, u32[]{:S(2)}) async-start(bf16[128,4,256]{0,2,1:T(8,128)(2,1)} %bitcast.7), calls=%async_computation.1 | async-start | bytes 524288 | tf_op jit(solution)/shard_map/all_to_all | solution.py:41
  24.0 1.3 %collective-permute-start.4 = (bf16[512,512]{1,0:T(8,128)(2,1)S(1)}, bf16[512,512]{1,0:T(8,128)(2,1)S(1)}, u32[]{:S(2)}, u32[]{:S(2)}) collective-permute-start(bf16[512,512]{1,0:T(8,128)(2,1)S(1)} %pad_maximum_fusion), channel_id=1, source_target_pairs={{0,4},{4,8},{8,12},{1,5},{5,9},{9,13},{2,6},{6,10},{10,14},{3,7},{... | collective-permute-start | bytes 1572872 | tf_op jit(solution)/shard_map/ppermute | solution.py:36
  25.3 0.0 copy-done.2
  25.4 0.1 reshape.94
  25.5 1.3 %collective-permute-start.3 = (bf16[256,512]{1,0:T(8,128)(2,1)S(1)}, bf16[256,512]{1,0:T(8,128)(2,1)S(1)}, u32[]{:S(2)}, u32[]{:S(2)}) collective-permute-start(bf16[256,512]{1,0:T(8,128)(2,1)S(1)} %fusion.22), channel_id=1, source_target_pairs={{0,8},{4,12},{1,9},{5,13},{2,10},{6,14},{3,11},{7,15},{16,24},{20,... | collective-permute-start | bytes 786440 | tf_op jit(solution)/shard_map/ppermute | solution.py:36
  26.8 14.3 %collective-permute-done.3 = bf16[256,512]{1,0:T(8,128)(2,1)S(1)} collective-permute-done((bf16[256,512]{1,0:T(8,128)(2,1)S(1)}, bf16[256,512]{1,0:T(8,128)(2,1)S(1)}, u32[]{:S(2)}, u32[]{:S(2)}) %collective-permute-start.3) | collective-permute-done | bytes 262176 | tf_op jit(solution)/shard_map/ppermute | solution.py:36
  41.1 0.0 collective-permute-done.4
  41.2 0.1 maximum_maximum_fusion
  41.2 2.6 %gather_fusion = bf16[28,128,512]{2,1,0:T(8,128)(2,1)} fusion(bf16[10,128,512]{2,1,0:T(8,128)(2,1)S(1)} %bitcast.71, s32[1024]{0:T(1024)S(1)} %pad_clamp_fusion), kind=kCustom, calls=%fused_computation | custom fusion | bytes 7340144 | tf_op jit(solution)/shard_map/while/body/eval_jaxpr/gather | solution.py:73
  43.9 3.6 %fusion.33 = (bf16[4,896,256]{2,1,0:T(8,128)(2,1)S(1)}, bf16[4,896,256]{2,1,0:T(8,128)(2,1)}) fusion(bf16[4,896,512]{2,1,0:T(8,128)(2,1)} %bitcast.72), kind=kLoop, calls=%fused_computation.52 | loop fusion | bytes 7340032 | tf_op jit(solution)/shard_map/while/body/eval_jaxpr/slice | solution.py:74
  47.5 3.6 %copy.27 = bf16[4,896,256]{1,2,0:T(8,128)(2,1)} copy(bf16[4,896,256]{2,1,0:T(8,128)(2,1)} %get-tuple-element.18) | data formatting | bytes 3670016 | tf_op jit(solution)/shard_map/while/body/eval_jaxpr/slice | solution.py:75
  51.0 2.3 %copy.28 = bf16[4,896,256]{1,2,0:T(8,128)(2,1)} copy(bf16[4,896,256]{2,1,0:T(8,128)(2,1)S(1)} %get-tuple-element.17) | data formatting | bytes 3670016 | tf_op jit(solution)/shard_map/while/body/eval_jaxpr/slice | solution.py:74
  53.3 0.0 all-to-all-done.1
  53.3 0.0 copy-start.1
  53.3 2.6 %bitcast_reduce_fusion = (f32[4,2,128]{2,1,0:T(2,128)S(1)}, f32[4,2,896,128]{3,2,1,0:T(8,128)S(1)}) fusion(pred[4,896]{1,0:T(4,128)(4,1)S(1)} %bitcast.82, bf16[4,896,2,128]{1,3,2,0:T(8,128)(2,1)} %bitcast.73, bf16[4,128,2,128]{1,3,2,0:T(8,128)(2,1)S(1)} %bitcast.80), kind=kOutput, calls=%fused_computation.2 | convolution fusion | flops 237632512 | bytes 5774848 | tf_op jit(solution)/shard_map/while/body/eval_jaxpr/qthd,qkhd->qhtk/dot_general | solution.py:77
  56.0 1.1 %fusion.1 = f32[4,2,128]{2,1,0:T(2,128)S(1)} fusion(f32[4,2,896,128]{3,2,1,0:T(8,128)S(1)} %get-tuple-element.32, f32[4,2,128]{2,1,0:T(2,128)S(1)} %get-tuple-element.30, pred[4,896]{1,0:T(4,128)(4,1)S(1)} %bitcast.83), kind=kLoop, calls=%fused_computation.5 | loop fusion | flops 3668992 | bytes 3681792 | tf_op jit(solution)/shard_map/while/body/eval_jaxpr/reduce_sum | solution.py:84
  57.1 0.0 copy-done.1
  57.1 1.3 %fusion.18 = bf16[4,128,2,128]{1,3,2,0:T(8,128)(2,1)S(1)} fusion(bf16[4,896,2,128]{1,3,2,0:T(8,128)(2,1)S(1)} %bitcast.77, f32[4,2,896,128]{3,2,1,0:T(8,128)S(1)} %get-tuple-element.32, f32[4,2,128]{2,1,0:T(2,128)S(1)} %get-tuple-element.30, pred[4,896]{1,0:T(4,128)(4,1)S(1)} %bitcast.84, f32[2,128]{1,0:T(2,128)S(1)} %broadcast_add_fusion, ...), kind=kOutput, calls=%fused_computation.16 | convolution fusion | flops 238944256 | bytes 5779968 | tf_op jit(solution)/shard_map/while/body/eval_jaxpr/qhtk,qkhd->qthd/dot_general | solution.py:86
  58.4 12.3 %all_to_all.54 = bf16[4,128,256]{1,2,0:T(8,128)(2,1)S(1)} all-to-all(bf16[4,128,256]{1,2,0:T(8,128)(2,1)S(1)} %bitcast.81), channel_id=1, replica_groups=mesh['groups'=2,'span'=4,'head'=4] {'head'}, dimensions={0} | all-to-all | bytes 524288 | tf_op jit(solution)/shard_map/all_to_all | solution.py:94
  70.7 0.8 %copy.39 = bf16[128,1024]{1,0:T(8,128)(2,1)} copy(bf16[128,1024]{0,1:T(8,128)(2,1)S(1)} %bitcast.78) | data formatting | bytes 524288 | tf_op jit(solution)/shard_map/all_to_all | solution.py:94
  (16 shorter events, 0.2 us)
Async XLA Ops:
  0.0 13.0 %copy-start = (bf16[256,256]{1,0:T(8,128)(2,1)S(1)}, bf16[256,256]{1,0:T(8,128)(2,1)}, u32[]{:S(2)}) copy-start(bf16[256,256]{1,0:T(8,128)(2,1)} %param.11) | copy-start | bytes 393220
  0.0 25.3 %copy-start.2 = (s32[4,7]{1,0:T(4,128)S(1)}, s32[4,7]{1,0:T(4,128)}, u32[]{:S(2)}) copy-start(s32[4,7]{1,0:T(4,128)} %param.9) | copy-start | bytes 340
  2.0 18.5 %all-to-all-start = ((bf16[128,4,256]{2,0,1:T(8,128)(2,1)}), bf16[128,4,256]{2,0,1:T(8,128)(2,1)S(1)}, u32[]{:S(2)}, u32[]{:S(2)}) async-start(bf16[128,4,256]{2,0,1:T(8,128)(2,1)} %copy.26), calls=%async_computation | async-start | bytes 524288 | tf_op jit(solution)/shard_map/all_to_all | solution.py:43
  7.7 7.4 %collective-permute-start = (bf16[128,256]{1,0:T(8,128)(2,1)S(1)}, bf16[128,256]{1,0:T(8,128)(2,1)S(1)}, u32[]{:S(2)}, u32[]{:S(2)}) collective-permute-start(bf16[128,256]{1,0:T(8,128)(2,1)S(1)} %get-tuple-element.28), channel_id=1, source_target_pairs={{0,3},{1,0},{2,1},{3,2},{4,7},{5,4},{6,5},{7,6},{8,11},{9,8},{10,9... | collective-permute-start | bytes 196616 | tf_op jit(solution)/shard_map/ppermute | solution.py:23
  11.0 9.4 %collective-permute-start.1 = (bf16[128,256]{1,0:T(8,128)(2,1)S(1)}, bf16[128,256]{1,0:T(8,128)(2,1)S(1)}, u32[]{:S(2)}, u32[]{:S(2)}) collective-permute-start(bf16[128,256]{1,0:T(8,128)(2,1)S(1)} %get-tuple-element.20), channel_id=1, source_target_pairs={{0,2},{1,3},{2,0},{3,1},{4,6},{5,7},{6,4},{7,5},{8,10},{9,11},{10,... | collective-permute-start | bytes 196616 | tf_op jit(solution)/shard_map/ppermute | solution.py:23
  11.0 9.4 %collective-permute-start.2 = (bf16[128,256]{1,0:T(8,128)(2,1)S(1)}, bf16[128,256]{1,0:T(8,128)(2,1)S(1)}, u32[]{:S(2)}, u32[]{:S(2)}) collective-permute-start(bf16[128,256]{1,0:T(8,128)(2,1)S(1)} %get-tuple-element.19), channel_id=1, source_target_pairs={{0,1},{1,2},{2,3},{3,0},{4,5},{5,6},{6,7},{7,4},{8,9},{9,10},{10,1... | collective-permute-start | bytes 196616 | tf_op jit(solution)/shard_map/ppermute | solution.py:23
  20.6 32.8 %all-to-all-start.1 = ((bf16[128,4,256]{0,2,1:T(8,128)(2,1)}), bf16[128,4,256]{0,2,1:T(8,128)(2,1)S(1)}, u32[]{:S(2)}, u32[]{:S(2)}) async-start(bf16[128,4,256]{0,2,1:T(8,128)(2,1)} %bitcast.7), calls=%async_computation.1 | async-start | bytes 524288 | tf_op jit(solution)/shard_map/all_to_all | solution.py:41
  24.0 17.1 %collective-permute-start.4 = (bf16[512,512]{1,0:T(8,128)(2,1)S(1)}, bf16[512,512]{1,0:T(8,128)(2,1)S(1)}, u32[]{:S(2)}, u32[]{:S(2)}) collective-permute-start(bf16[512,512]{1,0:T(8,128)(2,1)S(1)} %pad_maximum_fusion), channel_id=1, source_target_pairs={{0,4},{4,8},{8,12},{1,5},{5,9},{9,13},{2,6},{6,10},{10,14},{3,7},{... | collective-permute-start | bytes 1572872 | tf_op jit(solution)/shard_map/ppermute | solution.py:36
  25.5 15.7 %collective-permute-start.3 = (bf16[256,512]{1,0:T(8,128)(2,1)S(1)}, bf16[256,512]{1,0:T(8,128)(2,1)S(1)}, u32[]{:S(2)}, u32[]{:S(2)}) collective-permute-start(bf16[256,512]{1,0:T(8,128)(2,1)S(1)} %fusion.22), channel_id=1, source_target_pairs={{0,8},{4,12},{1,9},{5,13},{2,10},{6,14},{3,11},{7,15},{16,24},{20,... | collective-permute-start | bytes 786440 | tf_op jit(solution)/shard_map/ppermute | solution.py:36
  53.3 3.8 %copy-start.1 = (bf16[4,896,256]{1,2,0:T(8,128)(2,1)S(1)}, bf16[4,896,256]{1,2,0:T(8,128)(2,1)}, u32[]{:S(2)}) copy-start(bf16[4,896,256]{1,2,0:T(8,128)(2,1)} %copy.27) | copy-start | bytes 5505028
